TPU v7x, 512 devices: a whole 4x8x8 slice. The times are simulated.
512 devices in a mesh: gx: 64 (over z_lo, y, core), gy: 8 (over x, z_hi).
Axes of the slice: x: 4, y: 8, z: 8 (z_hi: 2, z_lo: 4; z = z_hi * 4 + z_lo), core: 2. Of those that a mesh axis runs over, the one named last changes fastest.
Arguments:
- forward_field: bfloat16 [2560, 128, 128], P('gy', 'gx'), may hold values from -6 to 6
- adjoint_field: bfloat16 [2560, 128, 128], P('gy', 'gx'), may hold values from -6 to 6
- row_scale: float32 [2560, 128], P('gy', 'gx'), may hold values from 0.5 to 2
- station_block: bfloat16 [2560, 2560], P('gy'), may hold values from -0.15625 to 0.15625
- jacobian_block: bfloat16 [2560, 2560], P('gy'), may hold values from -0.15625 to 0.15625
- shock_stations: int32 [16], replicated, may hold values from 0 to 127, as said below
Outputs:
- forward_image: bfloat16 [2560, 128, 128], P('gy', 'gx')
- adjoint_image: bfloat16 [2560, 128, 128], P('gy', 'gx')
Inputs may be any that keep to these rules, and one draw needn't show every extreme that they name: `shock_stations`: station indices, repeats possible; station 0 and station 128 - 1 are always listed.
All inputs are finite; a program needn't handle non-finite values.
Results may differ from a plain program's by a relative error of at most 0.013.
Values may be sent and summed in bfloat16 or wider, within the bound.
A program may use at most 64 MiB of HBM per device.

v0:
```python
import jax
import jax.numpy as jnp
from jax import lax
from jax.sharding import PartitionSpec as P

far_coeff = 1.0 / 12.0
near_coeff = 8.0 / 12.0
shock_gain = 0.5


def with_halo(block, sides, width):
    for axis, dim in sides:
        count = lax.axis_size(axis)
        forward = [(i, i + 1) for i in range(count - 1)]
        backward = [(target, source) for source, target in forward]
        low = lax.ppermute(
            lax.slice_in_dim(block, block.shape[dim] - width, None, axis=dim), axis, forward
        )
        high = lax.ppermute(lax.slice_in_dim(block, 0, width, axis=dim), axis, backward)
        block = jnp.concatenate([low, block, high], axis=dim)
    return block


def streamwise(ext, count):
    values = ext.astype(jnp.float32)
    return (
        far_coeff * values[:, 0:count]
        - near_coeff * values[:, 1 : 1 + count]
        + near_coeff * values[:, 3 : 3 + count]
        - far_coeff * values[:, 4 : 4 + count]
    )


def transposed(ext, count):
    values = ext.astype(jnp.float32)
    return (
        far_coeff * values[:, 4 : 4 + count]
        - near_coeff * values[:, 3 : 3 + count]
        + near_coeff * values[:, 1 : 1 + count]
        - far_coeff * values[:, 0:count]
    )


def second_diff(ext, count):
    values = ext.astype(jnp.float32)
    return values[:, 1 : 1 + count] - 2.0 * values[:, 2 : 2 + count] + values[:, 3 : 3 + count]


def left_dot(matrix, other):
    return lax.dot_general(
        matrix, other, (((0,), (0,)), ((), ())), preferred_element_type=jnp.float32
    )


def local(forward_field, adjoint_field, row_scale, station_block, jacobian_block, shock_stations):
    own_rows = forward_field.shape[0]
    count = forward_field.shape[1]
    width = forward_field.shape[2]
    flat = count * width
    total_rows = station_block.shape[1]
    first = lax.axis_index("gx") * count
    station_ids = first - 2 + jnp.arange(count + 4, dtype=jnp.int32)
    sigma_ext = jnp.any(station_ids[:, None] == shock_stations[None, :], axis=1).astype(jnp.float32)
    sigma_own = sigma_ext[2 : 2 + count]
    pencils = lax.all_gather(forward_field, "gy", axis=0, tiled=True)
    pencil_ext = with_halo(pencils, (("gx", 1),), 2)
    slope = streamwise(pencil_ext, count).astype(jnp.bfloat16)
    centre = pencil_ext[:, 2 : 2 + count].reshape(total_rows, flat)
    dense = jnp.dot(station_block, centre, preferred_element_type=jnp.float32)
    flux = jnp.dot(
        jacobian_block, slope.reshape(total_rows, flat), preferred_element_type=jnp.float32
    )
    own_ext = lax.dynamic_slice_in_dim(pencil_ext, lax.axis_index("gy") * own_rows, own_rows, 0)
    w_ext = with_halo(adjoint_field, (("gx", 1),), 2)
    forward_out = row_scale[:, :, None] * dense.reshape(own_rows, count, width) + flux.reshape(
        own_rows, count, width
    )
    forward_out = forward_out + shock_gain * sigma_own[None, :, None] * second_diff(own_ext, count)
    back = transposed(w_ext, count).astype(jnp.bfloat16).reshape(own_rows, flat)
    scaled = (
        (row_scale[:, :, None] * adjoint_field.astype(jnp.float32))
        .astype(jnp.bfloat16)
        .reshape(own_rows, flat)
    )
    summed = lax.psum_scatter(
        (left_dot(station_block, scaled) + left_dot(jacobian_block, back)).astype(jnp.bfloat16),
        "gy",
        scatter_dimension=0,
        tiled=True,
    ).astype(jnp.float32)
    weighted = sigma_ext[None, :, None] * w_ext.astype(jnp.float32)
    adjoint_out = summed.reshape(own_rows, count, width) + shock_gain * second_diff(weighted, count)
    return (forward_out.astype(jnp.bfloat16), adjoint_out.astype(jnp.bfloat16))


def solution(mesh):
    in_specs = (
        P("gy", "gx", None),
        P("gy", "gx", None),
        P("gy", "gx"),
        P("gy", None),
        P("gy", None),
        P(),
    )
    out_specs = (P("gy", "gx", None), P("gy", "gx", None))
    return jax.shard_map(local, mesh=mesh, in_specs=in_specs, out_specs=out_specs, check_vma=False)
```

profile of v0, /device:TPU:8, one launch (start us, length us, event | category | flops | bytes accessed | tf_op | source)
XLA Modules:
  0.0 205.7 jit_solution(1199272171501167596)
XLA Ops:
  7.2 0.0 copy-start
  7.2 0.0 all-gather.2.cloned.1.call-start
  7.2 1.7 copy.57
  8.9 0.0 all-gather.2.cloned.1.call-update
  9.0 0.0 reduce-scatter.4.cloned.1.call-start
  9.0 0.9 copy.61
  10.0 1.9 collective-permute-start.2
  11.9 3.6 %collective-permute-start.3 = (bf16[320,2,128]{2,0,1:T(8,128)(2,1)S(1)}, bf16[320,2,128]{2,0,1:T(8,128)(2,1)S(1)}, u32[]{:S(2)}, u32[]{:S(2)}) collective-permute-start(bf16[320,2,128]{2,0,1:T(8,128)(2,1)S(1)} %copy.61), channel_id=1, source_target_pairs={{8,0},{16,8},{24,16},{32,24},{40,32},{48,40},{56,48},{64,56},{72,6... | collective-permute-start | bytes 491528 | tf_op jit(solution)/shard_map/ppermute | solution.py:19
  15.5 2.5 %fusion.41 = f32[256,2560]{1,0:T(8,128)S(1)} fusion(bf16[320,2560]{1,0:T(8,128)(2,1)} %param.9, f32[320,2]{0,1:T(2,128)} %param.8, bf16[320,2,128]{2,1,0:T(2,128)(2,1)} %param.7), kind=kOutput, calls=%fused_computation.45 | convolution fusion | flops 419676160 | bytes 4426240 | tf_op jit(solution)/shard_map/dot_general | solution.py:50
  18.0 0.0 collective-permute-done.2
  18.0 0.3 collective-permute-done.3
  18.4 0.1 maximum_convert_fusion
  18.4 0.0 copy-done
  18.4 0.9 fusion.1
  19.4 0.0 copy-start.5
  19.4 1.5 copy.71
  20.8 0.0 reduce-scatter.4.cloned.1.call-update
  20.9 66.9 %all-gather.2.cloned.1.call-done = bf16[2560,2,128]{2,0,1:T(8,128)(2,1)} async-done(((bf16[320,2,128]{2,0,1:T(8,128)(2,1)}), bf16[2560,2,128]{2,0,1:T(8,128)(2,1)}) %all-gather.2.cloned.1.call-update) | async-done | bytes 1310736 | tf_op jit(solution)/shard_map/all_gather | solution.py:65
  87.8 0.0 copy-start.1
  87.8 2.0 collective-permute-start
  89.8 0.0 copy-done.5
  89.8 0.2 compare_reduce_fusion
  90.0 3.6 %collective-permute-start.1 = (bf16[2560,2,128]{2,0,1:T(8,128)(2,1)}, bf16[2560,2,128]{2,0,1:T(8,128)(2,1)}, u32[]{:S(2)}, u32[]{:S(2)}) collective-permute-start(bf16[2560,2,128]{2,0,1:T(8,128)(2,1)} %all-gather.2.cloned.1.call-done), channel_id=1, source_target_pairs={{8,0},{16,8},{24,16},{32,24},{40,32},{48,40},{56,48},{64,56},{72,6... | collective-permute-start | bytes 3932168 | tf_op jit(solution)/shard_map/ppermute | solution.py:19
  93.7 0.1 slice_multiply_fusion.10
  93.8 1.1 broadcast_multiply_fusion
  94.8 0.0 copy-done.1
  94.9 1.4 copy.58
  96.3 87.8 %reduce-scatter.4.cloned.1.call-done = bf16[320,256]{1,0:T(8,128)(2,1)} async-done(((bf16[2560,256]{1,0:T(8,128)(2,1)}), bf16[320,256]{1,0:T(8,128)(2,1)}) %reduce-scatter.4.cloned.1.call-update) | async-done | bytes 163856 | tf_op jit(solution)/shard_map/reduce_scatter | solution.py:85
  184.1 1.3 fusion.29
  185.5 0.8 copy.70
  186.3 0.0 collective-permute-done
  186.3 1.4 constant_dynamic-update-slice_fusion.2
  187.7 0.2 constant_dynamic-update-slice_fusion.1
  187.9 0.0 collective-permute-done.1
  187.9 1.5 constant_dynamic-update-slice_fusion
  189.4 0.5 convert_element_type.42
  189.9 1.0 dynamic-slice_convert_fusion
  191.0 1.8 fusion.3
  192.8 1.6 copy.59
  194.4 0.0 copy-start.2
  194.4 0.0 copy-start.3
  194.4 0.0 copy-start.4
  194.4 0.6 convolution_bitcast_fusion
  195.1 0.8 copy-done.2
  195.8 0.4 copy-done.3
  196.2 0.0 copy-done.4
  196.2 1.8 fusion.24
  198.0 0.8 copy.69
  (2 shorter events, 0.0 us)
Async XLA Ops:
  7.2 11.3 %copy-start = (bf16[320,2560]{1,0:T(8,128)(2,1)S(1)}, bf16[320,2560]{1,0:T(8,128)(2,1)}, u32[]{:S(2)}) copy-start(bf16[320,2560]{1,0:T(8,128)(2,1)} %param.10) | copy-start | bytes 4915204
  7.2 80.6 %all-gather.2.cloned.1.call-start = ((), (), s32[]{:S(2)}) async-start(), calls=%async_computation.1 | async-start | bytes 1474560 | tf_op jit(solution)/shard_map/all_gather | solution.py:65
  9.0 175.2 %reduce-scatter.4.cloned.1.call-start = ((), (), s32[]{:S(2)}) async-start(), calls=%async_computation.2 | async-start | bytes 1474560 | tf_op jit(solution)/shard_map/reduce_scatter | solution.py:85
  10.0 8.1 %collective-permute-start.2 = (bf16[320,2,128]{2,0,1:T(8,128)(2,1)S(1)}, bf16[320,2,128]{2,0,1:T(8,128)(2,1)S(1)}, u32[]{:S(2)}, u32[]{:S(2)}) collective-permute-start(bf16[320,2,128]{2,0,1:T(8,128)(2,1)S(1)} %copy.61), channel_id=1, source_target_pairs={{0,8},{8,16},{16,24},{24,32},{32,40},{40,48},{48,56},{56,64},{64,7... | collective-permute-start | bytes 491528 | tf_op jit(solution)/shard_map/ppermute | solution.py:16
  11.9 6.5 %collective-permute-start.3 = (bf16[320,2,128]{2,0,1:T(8,128)(2,1)S(1)}, bf16[320,2,128]{2,0,1:T(8,128)(2,1)S(1)}, u32[]{:S(2)}, u32[]{:S(2)}) collective-permute-start(bf16[320,2,128]{2,0,1:T(8,128)(2,1)S(1)} %copy.61), channel_id=1, source_target_pairs={{8,0},{16,8},{24,16},{32,24},{40,32},{48,40},{56,48},{64,56},{72,6... | collective-permute-start | bytes 491528 | tf_op jit(solution)/shard_map/ppermute | solution.py:19
  19.4 70.5 %copy-start.5 = (s32[16]{0:T(128)S(1)}, s32[16]{0:T(128)}, u32[]{:S(2)}) copy-start(s32[16]{0:T(128)} %param.11) | copy-start | bytes 196
  87.8 7.1 %copy-start.1 = (bf16[2560,2,128]{2,0,1:T(8,128)(2,1)S(1)}, bf16[2560,2,128]{2,0,1:T(8,128)(2,1)}, u32[]{:S(2)}) copy-start(bf16[2560,2,128]{2,0,1:T(8,128)(2,1)} %all-gather.2.cloned.1.call-done) | copy-start | bytes 3932164
  87.8 98.5 %collective-permute-start = (bf16[2560,2,128]{2,0,1:T(8,128)(2,1)}, bf16[2560,2,128]{2,0,1:T(8,128)(2,1)}, u32[]{:S(2)}, u32[]{:S(2)}) collective-permute-start(bf16[2560,2,128]{2,0,1:T(8,128)(2,1)} %all-gather.2.cloned.1.call-done), channel_id=1, source_target_pairs={{0,8},{8,16},{16,24},{24,32},{32,40},{40,48},{48,56},{56,64},{64,7... | collective-permute-start | bytes 3932168 | tf_op jit(solution)/shard_map/ppermute | solution.py:16
  90.0 97.9 %collective-permute-start.1 = (bf16[2560,2,128]{2,0,1:T(8,128)(2,1)}, bf16[2560,2,128]{2,0,1:T(8,128)(2,1)}, u32[]{:S(2)}, u32[]{:S(2)}) collective-permute-start(bf16[2560,2,128]{2,0,1:T(8,128)(2,1)} %all-gather.2.cloned.1.call-done), channel_id=1, source_target_pairs={{8,0},{16,8},{24,16},{32,24},{40,32},{48,40},{56,48},{64,56},{72,6... | collective-permute-start | bytes 3932168 | tf_op jit(solution)/shard_map/ppermute | solution.py:19
  194.4 1.4 copy-start.2
  194.4 1.8 copy-start.3
  194.4 1.8 copy-start.4
Sparse Core Ops, SparseCore 0:
  11.8 75.9 all-gather.1
  92.3 91.7 reduce-scatter.3
where the time goes:
time: 206 us
  waiting for transfers between devices  155 us (75%)
  between operations  14.2 us (7%)
  local copies, waits for them, and re-layouts  13.1 us (6%)
  starting transfers between devices  11.3 us (5%)
  other arithmetic  6.16 us (3%)
  matrix products  5.84 us (3%)
    reduce_scatter x1, waiting for transfers between devices, local(): lax.psum_scatter((left_dot(station_block, scaled) + left_dot(jacobian_blo...  87.8 us
    all_gather x1, waiting for transfers between devices, local(): pencils = lax.all_gather(forward_field, 'gy', axis=0, tiled=True)  66.9 us
    unnamed x19, local copies, waits for them, and re-layouts  8.54 us
    ppermute x2, starting transfers between devices, with_halo(): lax.ppermute(lax.slice_in_dim(block, 0, width, axis=dim), axis, backward)  7.28 us
  transfers between devices with their start and end apart: 6, of which 3 were waited for; matrix products, arithmetic and copies ran while one was open for 6% of the time, Pallas kernels for 0%

commit v1 on v0

--- a/solution.py
+++ b/solution.py
@@ -62,7 +62,9 @@
     station_ids = first - 2 + jnp.arange(count + 4, dtype=jnp.int32)
     sigma_ext = jnp.any(station_ids[:, None] == shock_stations[None, :], axis=1).astype(jnp.float32)
     sigma_own = sigma_ext[2 : 2 + count]
-    pencils = lax.all_gather(forward_field, "gy", axis=0, tiled=True)
+    pencils = jnp.concatenate(
+        lax.all_to_all(jnp.stack([forward_field] * lax.axis_size("gy")), "gy", 0, 0), axis=0
+    )
     pencil_ext = with_halo(pencils, (("gx", 1),), 2)
     slope = streamwise(pencil_ext, count).astype(jnp.bfloat16)
     centre = pencil_ext[:, 2 : 2 + count].reshape(total_rows, flat)

time: 206 us -> 167 us (0.81)
  waiting for transfers between devices: 155 us -> 96.7 us
  starting transfers between devices: 11.3 us -> 24 us
  other arithmetic: 6.16 us -> 11.2 us
    all_gather x1 -> x0, waiting for transfers between devices: 66.9 us -> none  [local(): pencils = lax.all_gather(forward_field, 'gy', axis=0, tiled=True)]
    all_to_all x0 -> x1, waiting for transfers between devices: none -> 14.8 us  [local(): lax.all_to_all(jnp.stack([forward_field] * lax.axis_size('gy')), 'gy', 0, 0)]
    all_to_all x0 -> x1, starting transfers between devices: none -> 12.9 us  [local(): lax.all_to_all(jnp.stack([forward_field] * lax.axis_size('gy')), 'gy', 0, 0)]
    reduce_scatter x1, waiting for transfers between devices: 87.8 us -> 81.9 us  [local(): lax.psum_scatter((left_dot(station_block, scaled) + left_dot(jacobian_blo...]
    concatenate x0 -> x1, other arithmetic: none -> 3.77 us  [with_halo(): block = jnp.concatenate([low, block, high], axis=dim)]
    another operation x0 -> x1, local copies, waits for them, and re-layouts: none -> 2.65 us  [local(): jnp.stack([forward_field] * lax.axis_size('gy'))]
    dot_general x0 -> x1, local copies, waits for them, and re-layouts: none -> 2.52 us  [local(): dense = jnp.dot(station_block, centre, preferred_element_type=jnp.float32)]
    unnamed x19, local copies, waits for them, and re-layouts: 8.54 us -> 6.43 us
  transfers between devices with their start and end apart: 6 -> 6, of which waited for: 3 -> 2; matrix products, arithmetic and copies ran while one was open for 6% -> 12% of each run, Pallas kernels for 0% -> 0%
where the time goes in v1:
time: 167 us; the launch traced here: 166 us
  waiting for transfers between devices  96.7 us (58%)
  starting transfers between devices  24 us (14%)
  local copies, waits for them, and re-layouts  14.5 us (9%)
  between operations  14.2 us (9%)
  other arithmetic  11.2 us (7%)
  matrix products  5.59 us (3%)
    reduce_scatter x1, waiting for transfers between devices, local(): lax.psum_scatter((left_dot(station_block, scaled) + left_dot(jacobian_blo...  81.9 us
    all_to_all x1, waiting for transfers between devices, local(): lax.all_to_all(jnp.stack([forward_field] * lax.axis_size('gy')), 'gy', 0, 0)  14.8 us
    all_to_all x1, starting transfers between devices, local(): lax.all_to_all(jnp.stack([forward_field] * lax.axis_size('gy')), 'gy', 0, 0)  12.9 us
    ppermute x2, starting transfers between devices, with_halo(): lax.ppermute(lax.slice_in_dim(block, 0, width, axis=dim), axis, backward)  7.29 us
    unnamed x19, local copies, waits for them, and re-layouts  6.43 us
    dot_general x2, matrix products, left_dot(): lax.dot_general(matrix, other, (((0,), (0,)), ((), ())), preferred_elemen...  4.35 us
    ppermute x2, starting transfers between devices, with_halo(): lax.ppermute(lax.slice_in_dim(block, block.shape[dim] - width, None, axis...  3.83 us
    concatenate x1, other arithmetic, with_halo(): block = jnp.concatenate([low, block, high], axis=dim)  3.77 us
  transfers between devices with their start and end apart: 6, of which 2 were waited for; matrix products, arithmetic and copies ran while one was open for 12% of the time, Pallas kernels for 0%

profile of v1, /device:TPU:8, one launch (start us, length us, event | category | flops | bytes accessed | tf_op | source)
XLA Modules:
  0.0 166.3 jit_solution(9959690324860029389)
XLA Ops:
  7.2 0.0 copy-start
  7.2 1.1 copy.62
  8.2 1.9 %collective-permute-start.2 = (bf16[320,2,128]{2,0,1:T(8,128)(2,1)S(1)}, bf16[320,2,128]{2,0,1:T(8,128)(2,1)S(1)}, u32[]{:S(2)}, u32[]{:S(2)}) collective-permute-start(bf16[320,2,128]{2,0,1:T(8,128)(2,1)S(1)} %copy.62), channel_id=1, source_target_pairs={{0,8},{8,16},{16,24},{24,32},{32,40},{40,48},{48,56},{56,64},{64,7... | collective-permute-start | bytes 491528 | tf_op jit(solution)/shard_map/ppermute | solution.py:16
  10.2 3.6 %collective-permute-start.3 = (bf16[320,2,128]{2,0,1:T(8,128)(2,1)S(1)}, bf16[320,2,128]{2,0,1:T(8,128)(2,1)}, u32[]{:S(2)}, u32[]{:S(2)}) collective-permute-start(bf16[320,2,128]{2,0,1:T(8,128)(2,1)S(1)} %copy.62), channel_id=1, source_target_pairs={{8,0},{16,8},{24,16},{32,24},{40,32},{48,40},{56,48},{64,56},{72,6... | collective-permute-start | bytes 491528 | tf_op jit(solution)/shard_map/ppermute | solution.py:19
  13.8 2.6 %stack.2 = bf16[8,320,2,128]{3,2,1,0:T(2,128)(2,1)} broadcast(bf16[320,2,128]{2,1,0:T(2,128)(2,1)} %param.6), dimensions={1,2,3} | broadcast | bytes 1474560 | tf_op jit(solution)/shard_map/stack | solution.py:66
  16.5 0.0 copy-start.4
  16.5 0.0 copy-start.5
  16.5 12.9 %all-to-all-start = ((bf16[8,320,2,128]{3,2,1,0:T(2,128)(2,1)}), bf16[8,320,2,128]{3,2,1,0:T(2,128)(2,1)S(1)}, u32[]{:S(2)}, u32[]{:S(2)}) async-start(bf16[8,320,2,128]{3,2,1,0:T(2,128)(2,1)} %stack.2), calls=%async_computation | async-start | bytes 2621440 | tf_op jit(solution)/shard_map/all_to_all | solution.py:66
  29.4 0.0 reduce-scatter.4.cloned.1.call-start
  29.4 0.0 copy-done.4
  29.4 0.0 copy-done.5
  29.4 2.4 %fusion.32 = f32[256,2560]{1,0:T(8,128)S(1)} fusion(bf16[320,2560]{1,0:T(8,128)(2,1)} %param.9, f32[320,2]{0,1:T(2,128)S(1)} %copy-done.5, bf16[320,2,128]{2,1,0:T(2,128)(2,1)S(1)} %copy-done.4), kind=kOutput, calls=%fused_computation.46 | convolution fusion | flops 419676160 | bytes 4426240 | tf_op jit(solution)/shard_map/dot_general | solution.py:50
  31.8 0.0 collective-permute-done.2
  31.8 0.0 collective-permute-done.3
  31.8 1.0 maximum_convert_fusion
  32.8 0.0 copy-done
  32.8 2.0 %fusion.1 = bf16[2560,256]{0,1:T(8,128)(2,1)} fusion(f32[256,2560]{1,0:T(8,128)S(1)} %fusion.32, bf16[320,2560]{1,0:T(8,128)(2,1)S(1)} %copy-done, f32[320,6,128]{2,0,1:T(8,128)S(1)} %maximum_convert_fusion), kind=kOutput, calls=%fused_computation.3 | convolution fusion | flops 421396480 | bytes 6881280 | tf_op jit(solution)/shard_map/dot_general | solution.py:50
  34.8 2.4 %copy.72 = bf16[2560,256]{1,0:T(8,128)(2,1)} copy(bf16[2560,256]{0,1:T(8,128)(2,1)} %fusion.1) | data formatting | bytes 2621440
  37.2 0.0 reduce-scatter.4.cloned.1.call-update
  37.3 0.0 copy-start.6
  37.3 14.8 %all-to-all-done = bf16[8,320,2,128]{3,2,1,0:T(2,128)(2,1)S(1)} async-done(((bf16[8,320,2,128]{3,2,1,0:T(2,128)(2,1)}), bf16[8,320,2,128]{3,2,1,0:T(2,128)(2,1)S(1)}, u32[]{:S(2)}, u32[]{:S(2)}) %all-to-all-start) | async-done | bytes 1310752 | tf_op jit(solution)/shard_map/all_to_all | solution.py:66
  52.1 1.4 copy.59
  53.4 1.9 %collective-permute-start = (bf16[2560,2,128]{2,0,1:T(8,128)(2,1)}, bf16[2560,2,128]{2,0,1:T(8,128)(2,1)}, u32[]{:S(2)}, u32[]{:S(2)}) collective-permute-start(bf16[2560,2,128]{2,0,1:T(8,128)(2,1)} %bitcast.3), channel_id=1, source_target_pairs={{0,8},{8,16},{16,24},{24,32},{32,40},{40,48},{48,56},{56,64},{64,7... | collective-permute-start | bytes 3932168 | tf_op jit(solution)/shard_map/ppermute | solution.py:16
  55.4 3.6 %collective-permute-start.1 = (bf16[2560,2,128]{2,0,1:T(8,128)(2,1)}, bf16[2560,2,128]{2,0,1:T(8,128)(2,1)}, u32[]{:S(2)}, u32[]{:S(2)}) collective-permute-start(bf16[2560,2,128]{2,0,1:T(8,128)(2,1)} %bitcast.3), channel_id=1, source_target_pairs={{8,0},{16,8},{24,16},{32,24},{40,32},{48,40},{56,48},{64,56},{72,6... | collective-permute-start | bytes 3932168 | tf_op jit(solution)/shard_map/ppermute | solution.py:19
  59.0 0.0 copy-done.6
  59.0 0.2 compare_reduce_fusion
  59.2 0.1 slice_multiply_fusion.10
  59.3 2.0 %broadcast_multiply_fusion = f32[320,6,128]{2,0,1:T(8,128)} fusion(f32[6]{0:T(128)S(1)} %convert_element_type.44, bf16[320,2,128]{2,0,1:T(8,128)(2,1)} %collective-permute-done.3, bf16[320,2,128]{2,0,1:T(8,128)(2,1)S(1)} %copy.62, bf16[320,2,128]{2,0,1:T(8,128)(2,1)S(1)} %collective-permute-done.2), kind=kLoop, calls=%fused_computation.21 | loop fusion | flops 983040 | bytes 1474584 | tf_op jit(solution)/shard_map/mul | solution.py:93
  61.3 1.2 copy.93
  62.5 0.0 copy-start.1
  62.5 2.5 %copy.58 = bf16[256,2560]{1,0:T(8,128)(2,1)} copy(bf16[256,2560]{0,1:T(8,128)(2,1)} %bitcast.58) | data formatting | bytes 2621440 | tf_op jit(solution)/shard_map/dot_general | solution.py:71
  65.1 81.9 %reduce-scatter.4.cloned.1.call-done = bf16[320,256]{1,0:T(8,128)(2,1)} async-done(((bf16[2560,256]{1,0:T(8,128)(2,1)}), bf16[320,256]{1,0:T(8,128)(2,1)}) %reduce-scatter.4.cloned.1.call-update) | async-done | bytes 163856 | tf_op jit(solution)/shard_map/reduce_scatter | solution.py:87
  147.0 0.0 copy-done.1
  147.0 1.0 fusion.20
  148.0 0.8 copy.71
  148.8 0.0 collective-permute-done
  148.8 0.0 collective-permute-done.1
  148.8 3.8 %pad_maximum_fusion = (bf16[2560,6,128]{2,0,1:T(8,128)(2,1)}, f32[2560,6,128]{2,0,1:T(8,128)S(1)}) fusion(bf16[2560,2,128]{2,0,1:T(8,128)(2,1)} %collective-permute-done.1, bf16[2560,2,128]{2,0,1:T(8,128)(2,1)} %bitcast.3, bf16[2560,2,128]{2,0,1:T(8,128)(2,1)} %collective-permute-done), kind=kLoop, calls=%fused_computation.1 | loop fusion | flops 5898240 | bytes 15728640 | tf_op jit(solution)/shard_map/concatenate | solution.py:20
  152.6 1.8 %fusion.3 = bf16[2560,2,128]{2,0,1:T(8,128)(2,1)} fusion(f32[2560,6,128]{2,0,1:T(8,128)S(1)} %get-tuple-element.13), kind=kLoop, calls=%fused_computation.6 | loop fusion | flops 5242880 | bytes 11796480 | tf_op jit(solution)/shard_map/convert_element_type | solution.py:69
  154.4 1.6 copy.60
  156.0 0.0 copy-start.2
  156.0 0.0 copy-start.3
  156.0 0.6 convolution_bitcast_fusion
  156.7 1.3 dynamic-slice_convert_fusion
  158.0 0.0 copy-done.2
  158.0 0.0 copy-done.3
  158.0 0.6 fusion.17
  158.7 0.8 copy.70
  (2 shorter events, 0.0 us)
Async XLA Ops:
  7.2 25.7 %copy-start = (bf16[320,2560]{1,0:T(8,128)(2,1)S(1)}, bf16[320,2560]{1,0:T(8,128)(2,1)}, u32[]{:S(2)}) copy-start(bf16[320,2560]{1,0:T(8,128)(2,1)} %param.10) | copy-start | bytes 4915204
  8.2 23.6 %collective-permute-start.2 = (bf16[320,2,128]{2,0,1:T(8,128)(2,1)S(1)}, bf16[320,2,128]{2,0,1:T(8,128)(2,1)S(1)}, u32[]{:S(2)}, u32[]{:S(2)}) collective-permute-start(bf16[320,2,128]{2,0,1:T(8,128)(2,1)S(1)} %copy.62), channel_id=1, source_target_pairs={{0,8},{8,16},{16,24},{24,32},{32,40},{40,48},{48,56},{56,64},{64,7... | collective-permute-start | bytes 491528 | tf_op jit(solution)/shard_map/ppermute | solution.py:16
  10.2 21.6 %collective-permute-start.3 = (bf16[320,2,128]{2,0,1:T(8,128)(2,1)S(1)}, bf16[320,2,128]{2,0,1:T(8,128)(2,1)}, u32[]{:S(2)}, u32[]{:S(2)}) collective-permute-start(bf16[320,2,128]{2,0,1:T(8,128)(2,1)S(1)} %copy.62), channel_id=1, source_target_pairs={{8,0},{16,8},{24,16},{32,24},{40,32},{48,40},{56,48},{64,56},{72,6... | collective-permute-start | bytes 491528 | tf_op jit(solution)/shard_map/ppermute | solution.py:19
  16.5 12.9 %copy-start.4 = (bf16[320,2,128]{2,1,0:T(2,128)(2,1)S(1)}, bf16[320,2,128]{2,1,0:T(2,128)(2,1)}, u32[]{:S(2)}) copy-start(bf16[320,2,128]{2,1,0:T(2,128)(2,1)} %param.7) | copy-start | bytes 491524
  16.5 12.9 %copy-start.5 = (f32[320,2]{0,1:T(2,128)S(1)}, f32[320,2]{0,1:T(2,128)}, u32[]{:S(2)}) copy-start(f32[320,2]{0,1:T(2,128)} %param.8) | copy-start | bytes 7684
  16.5 35.6 %all-to-all-start = ((bf16[8,320,2,128]{3,2,1,0:T(2,128)(2,1)}), bf16[8,320,2,128]{3,2,1,0:T(2,128)(2,1)S(1)}, u32[]{:S(2)}, u32[]{:S(2)}) async-start(bf16[8,320,2,128]{3,2,1,0:T(2,128)(2,1)} %stack.2), calls=%async_computation | async-start | bytes 2621440 | tf_op jit(solution)/shard_map/all_to_all | solution.py:66
  29.4 117.6 %reduce-scatter.4.cloned.1.call-start = ((), (), s32[]{:S(2)}) async-start(), calls=%async_computation.2 | async-start | bytes 1474560 | tf_op jit(solution)/shard_map/reduce_scatter | solution.py:87
  37.3 21.8 %copy-start.6 = (s32[16]{0:T(128)S(1)}, s32[16]{0:T(128)}, u32[]{:S(2)}) copy-start(s32[16]{0:T(128)} %param.11) | copy-start | bytes 196
  53.4 95.4 %collective-permute-start = (bf16[2560,2,128]{2,0,1:T(8,128)(2,1)}, bf16[2560,2,128]{2,0,1:T(8,128)(2,1)}, u32[]{:S(2)}, u32[]{:S(2)}) collective-permute-start(bf16[2560,2,128]{2,0,1:T(8,128)(2,1)} %bitcast.3), channel_id=1, source_target_pairs={{0,8},{8,16},{16,24},{24,32},{32,40},{40,48},{48,56},{56,64},{64,7... | collective-permute-start | bytes 3932168 | tf_op jit(solution)/shard_map/ppermute | solution.py:16
  55.4 93.4 %collective-permute-start.1 = (bf16[2560,2,128]{2,0,1:T(8,128)(2,1)}, bf16[2560,2,128]{2,0,1:T(8,128)(2,1)}, u32[]{:S(2)}, u32[]{:S(2)}) collective-permute-start(bf16[2560,2,128]{2,0,1:T(8,128)(2,1)} %bitcast.3), channel_id=1, source_target_pairs={{8,0},{16,8},{24,16},{32,24},{40,32},{48,40},{56,48},{64,56},{72,6... | collective-permute-start | bytes 3932168 | tf_op jit(solution)/shard_map/ppermute | solution.py:19
  62.5 84.4 %copy-start.1 = (f32[320,6,128]{2,0,1:T(8,128)S(1)}, f32[320,6,128]{2,0,1:T(8,128)}, u32[]{:S(2)}) copy-start(f32[320,6,128]{2,0,1:T(8,128)} %broadcast_multiply_fusion) | copy-start | bytes 2949124
  156.0 2.0 %copy-start.2 = (bf16[320,2560]{1,0:T(8,128)(2,1)S(1)}, bf16[320,2560]{1,0:T(8,128)(2,1)}, u32[]{:S(2)}) copy-start(bf16[320,2560]{1,0:T(8,128)(2,1)} %param.9) | copy-start | bytes 4915204
  156.0 2.0 %copy-start.3 = (bf16[256,2560]{1,0:T(8,128)(2,1)S(1)}, bf16[256,2560]{1,0:T(8,128)(2,1)}, u32[]{:S(2)}) copy-start(bf16[256,2560]{1,0:T(8,128)(2,1)} %copy.58) | copy-start | bytes 3932164
Sparse Core Ops, SparseCore 0:
  37.4 109.5 reduce-scatter.3
